TPU v7x, 256 devices: a whole 4x4x8 slice. The times are simulated.
256 devices in a mesh: ep: 64 (over z, x, y_hi), tp: 4 (over y_lo, core).
Axes of the slice: x: 4, y: 4 (y_hi: 2, y_lo: 2; y = y_hi * 2 + y_lo), z: 8, core: 2. Of those that a mesh axis runs over, the one named last changes fastest.
Arguments:
- context: bfloat16 [8192, 4096], P('ep', 'tp'), may hold values from -6 to 6
- wo_proj: bfloat16 [4096, 4096], P('tp'), may hold values from -0.09375 to 0.09375
- residual: bfloat16 [8192, 4096], P(('ep', 'tp')), may hold values from -16 to 16
- norm_gain: bfloat16 [4096], replicated, may hold values from 0.25 to 1.75
- expert_ids: int32 [8192, 8], P(('ep', 'tp')), may hold values from 0 to 63, all different within a row; in each aligned block of 32 rows (0 to 31, 32 to 63, ...) at most 8 rows name the same one
- route_weights: float32 [8192, 8], P(('ep', 'tp')), may hold values from 0.1 to 1
- w_gate_up: bfloat16 [64, 2, 768, 4096], P('ep', None, 'tp'), may hold values from -0.09375 to 0.09375
- w_down: bfloat16 [64, 768, 4096], P('ep', 'tp'), may hold values from -0.21875 to 0.21875
Outputs:
- layer_out: bfloat16 [8192, 4096], P(('ep', 'tp'))
Inputs may be any that keep to these rules, and one draw needn't show every extreme that they name: `expert_ids`: within the routes of one device's 32 tokens no expert is named more than 8 times, a bound that some block reaches; a token names 8 different experts.
All inputs are finite; a program needn't handle non-finite values.
Results may differ from a plain program's by a relative error of at most 0.0085.
Values may be sent and summed in bfloat16 or wider, within the bound.
A program may use at most 128 MiB of HBM per device.

v0:
```python
import jax
import jax.numpy as jnp
from jax import lax
from jax.sharding import PartitionSpec as P


def local(context, wo_proj, residual, norm_gain, expert_ids, route_weights, w_gate_up, w_down):
    quarter_rows, model_width = residual.shape
    top_count = expert_ids.shape[1]
    exp_local = w_gate_up.shape[0]
    ep_size = lax.axis_size("ep")
    experts = exp_local * ep_size
    capacity = max(2, min(quarter_rows, 2 * quarter_rows * top_count // experts))
    gate_up_full = lax.all_gather(w_gate_up, "tp", axis=2, tiled=True)
    down_full = lax.all_gather(w_down, "tp", axis=1, tiled=True)
    attn = lax.psum_scatter(
        jnp.dot(context, wo_proj, preferred_element_type=jnp.float32),
        "tp",
        scatter_dimension=0,
        tiled=True,
    )
    hidden = residual.astype(jnp.float32) + attn
    inverse_rms = lax.rsqrt(jnp.mean(hidden * hidden, axis=1, keepdims=True) + 1e-06)
    normed = (hidden * inverse_rms * norm_gain.astype(jnp.float32)).astype(jnp.bfloat16)
    flat_ids = expert_ids.reshape(-1)
    onehot = (flat_ids[:, None] == jnp.arange(experts, dtype=jnp.int32)[None, :]).astype(jnp.int32)
    before = jnp.cumsum(onehot, axis=0, dtype=jnp.int32) - onehot
    position = jnp.sum(before * onehot, axis=1, dtype=jnp.int32)
    slot_ids = flat_ids * capacity + position
    slot_range = jnp.arange(experts * capacity, dtype=jnp.int32)
    selected = slot_range[:, None] == slot_ids[None, :]
    placement = jnp.any(
        selected.reshape(experts * capacity, quarter_rows, top_count), axis=2
    ).astype(jnp.bfloat16)
    send_rows = jnp.dot(placement, normed, preferred_element_type=jnp.float32).astype(jnp.bfloat16)
    send_rows = send_rows.reshape(ep_size, exp_local * capacity, model_width)
    received = lax.all_to_all(send_rows, "ep", split_axis=0, concat_axis=0, tiled=True)
    received = received.reshape(ep_size, exp_local, capacity, model_width)
    gate = jnp.einsum(
        "sjcd,jfd->sjcf", received, gate_up_full[:, 0], preferred_element_type=jnp.float32
    )
    up_proj = jnp.einsum(
        "sjcd,jfd->sjcf", received, gate_up_full[:, 1], preferred_element_type=jnp.float32
    )
    activated = (jax.nn.silu(gate) * up_proj).astype(jnp.bfloat16)
    expert_out = jnp.einsum(
        "sjcf,jfd->sjcd", activated, down_full, preferred_element_type=jnp.float32
    ).astype(jnp.bfloat16)
    returned = lax.all_to_all(
        expert_out.reshape(ep_size, exp_local * capacity, model_width),
        "ep",
        split_axis=0,
        concat_axis=0,
        tiled=True,
    )
    returned = returned.reshape(experts * capacity, model_width)
    token_slots = slot_ids.reshape(quarter_rows, top_count)
    mixture = jnp.zeros((quarter_rows, model_width), jnp.float32)
    for choice_index in range(top_count):
        picker = (slot_range[None, :] == token_slots[:, choice_index][:, None]).astype(jnp.bfloat16)
        picked = jnp.dot(picker, returned, preferred_element_type=jnp.float32)
        mixture = mixture + route_weights[:, choice_index : choice_index + 1] * picked
    return (hidden + mixture).astype(jnp.bfloat16)


def solution(mesh):
    in_specs = (
        P("ep", "tp"),
        P("tp", None),
        P(("ep", "tp"), None),
        P(),
        P(("ep", "tp"), None),
        P(("ep", "tp"), None),
        P("ep", None, "tp", None),
        P("ep", "tp", None),
    )
    out_specs = P(("ep", "tp"), None)
    return jax.shard_map(local, mesh=mesh, in_specs=in_specs, out_specs=out_specs, check_vma=False)
```

profile of v0, /device:TPU:1, one launch (start us, length us, event | category | flops | bytes accessed | tf_op | source)
XLA Modules:
  0.0 444.3 jit_solution(16430905282046604405)
XLA Ops:
  6.5 0.9 copy-done
  7.5 5.9 %fusion.47 = f32[128,4096]{1,0:T(8,128)} fusion(bf16[128,1024]{1,0:T(8,128)(2,1)S(1)} %copy-done, bf16[1024,4096]{1,0:T(8,128)(2,1)} %param.9), kind=kOutput, calls=%fused_computation.94 | convolution fusion | flops 1073741824 | bytes 10747904 | tf_op jit(solution)/shard_map/dot_general | solution.py:17
  13.5 0.7 all-gather.3.cloned.1.call-update
  14.3 0.7 all-gather.5.cloned.1.call-update
  15.3 0.6 reduce-window.6
  16.5 31.9 %reduce-scatter.2.cloned.1.call-done = f32[32,4096]{1,0:T(8,128)} async-done(((f32[128,4096]{1,0:T(8,128)}), f32[32,4096]{1,0:T(8,128)}) %reduce-scatter.2.cloned.1.call-update) | async-done | bytes 524304 | tf_op jit(solution)/shard_map/reduce_scatter | solution.py:16
  48.4 1.2 multiply_reduce_fusion
  49.6 2.4 fusion.7
  52.0 106.6 %all_to_all.10 = bf16[64,8,4096]{2,1,0:T(8,128)(2,1)} all-to-all(bf16[64,8,4096]{2,1,0:T(8,128)(2,1)S(1)} %fusion.7), channel_id=1, replica_groups=mesh['ep'=64,'tp'=4] {'ep'}, dimensions={0} | all-to-all | bytes 8388608 | tf_op jit(solution)/shard_map/all_to_all | solution.py:37
  158.6 53.6 %all-gather.3.cloned.1.call-done = bf16[1,2,768,4096]{3,2,1,0:T(8,128)(2,1)} async-done(((bf16[1,2,192,4096]{3,2,1,0:T(8,128)(2,1)}), bf16[1,2,768,4096]{3,2,1,0:T(8,128)(2,1)}) %all-gather.3.cloned.1.call-update) | async-done | bytes 12582928 | tf_op jit(solution)/shard_map/all_gather | solution.py:14
  212.2 7.1 %fusion.1 = f32[64,8,768]{2,1,0:T(8,128)S(1)} fusion(bf16[64,8,4096]{2,1,0:T(8,128)(2,1)} %all_to_all.10, bf16[1,2,768,4096]{3,2,1,0:T(8,128)(2,1)} %all-gather.3.cloned.1.call-done), kind=kOutput, calls=%fused_computation.3 | convolution fusion | flops 3221225472 | bytes 12058624 | tf_op jit(solution)/shard_map/sjcd,jfd->sjcf/dot_general | solution.py:39
  219.3 62.0 %all-gather.5.cloned.1.call-done = bf16[1,768,4096]{2,1,0:T(8,128)(2,1)} async-done(((bf16[1,192,4096]{2,1,0:T(8,128)(2,1)}), bf16[1,768,4096]{2,1,0:T(8,128)(2,1)}) %all-gather.5.cloned.1.call-update) | async-done | bytes 6291472 | tf_op jit(solution)/shard_map/all_gather | solution.py:15
  281.3 16.6 %fusion.4 = bf16[64,8,4096]{2,1,0:T(8,128)(2,1)} fusion(bf16[1,768,4096]{2,1,0:T(8,128)(2,1)} %all-gather.5.cloned.1.call-done, bf16[64,8,4096]{2,1,0:T(8,128)(2,1)} %all_to_all.10, bf16[1,2,768,4096]{3,2,1,0:T(8,128)(2,1)} %all-gather.3.cloned.1.call-done, f32[64,8,768]{2,1,0:T(8,128)S(1)} %fusion.1), kind=kOutput, calls=%fused_computation.6 | convolution fusion | flops 6446907392 | bytes 22544384 | tf_op jit(solution)/shard_map/sjcf,jfd->sjcd/dot_general | solution.py:46
  297.9 12.9 %all-to-all-start.1 = ((bf16[64,8,4096]{2,1,0:T(8,128)(2,1)}), bf16[64,8,4096]{2,1,0:T(8,128)(2,1)}, u32[]{:S(2)}, u32[]{:S(2)}) async-start(bf16[64,8,4096]{2,1,0:T(8,128)(2,1)} %fusion.4), calls=%async_computation.2 | async-start | bytes 8388608 | tf_op jit(solution)/shard_map/all_to_all | solution.py:49
  310.8 0.3 slice_reduce_fusion.1
  311.2 101.4 %all-to-all-done.1 = bf16[64,8,4096]{2,1,0:T(8,128)(2,1)} async-done(((bf16[64,8,4096]{2,1,0:T(8,128)(2,1)}), bf16[64,8,4096]{2,1,0:T(8,128)(2,1)}, u32[]{:S(2)}, u32[]{:S(2)}) %all-to-all-start.1) | async-done | bytes 4194336 | tf_op jit(solution)/shard_map/all_to_all | solution.py:49
  412.5 3.0 convolution_multiply_fusion.7
  415.6 3.0 fusion.15
  418.6 3.0 fusion.14
  421.7 3.0 fusion.13
  424.7 3.0 fusion.12
  427.8 3.1 fusion.11
  430.9 3.0 fusion.10
  434.0 3.8 fusion.16
  (29 shorter events, 1.1 us)
Async XLA Ops:
  6.5 1.0 copy-start
  6.5 41.9 %reduce-scatter.2.cloned.1.call-start = ((), (), s32[]{:S(2)}) async-start(), calls=%async_computation.3 | async-start | bytes 2621440 | tf_op jit(solution)/shard_map/reduce_scatter | solution.py:16
  13.4 1.5 copy-start.4
  13.4 1.8 copy-start.3
  13.4 35.0 %copy-start.2 = (bf16[32,4096]{1,0:T(8,128)(2,1)S(1)}, bf16[32,4096]{1,0:T(8,128)(2,1)}, u32[]{:S(2)}) copy-start(bf16[32,4096]{1,0:T(8,128)(2,1)} %param.10) | copy-start | bytes 786436
  13.5 198.7 %all-gather.3.cloned.1.call-start = ((), (), s32[]{:S(2)}) async-start(), calls=%async_computation.4 | async-start | bytes 15728640 | tf_op jit(solution)/shard_map/all_gather | solution.py:14
  14.2 267.1 %all-gather.5.cloned.1.call-start = ((), (), s32[]{:S(2)}) async-start(), calls=%async_computation.5 | async-start | bytes 7864320 | tf_op jit(solution)/shard_map/all_gather | solution.py:15
  297.9 13.2 %copy-start.5 = (f32[32,8]{0,1:T(8,128)S(1)}, f32[32,8]{0,1:T(8,128)}, u32[]{:S(2)}) copy-start(f32[32,8]{0,1:T(8,128)} %param.13) | copy-start | bytes 3076
  297.9 114.6 %all-to-all-start.1 = ((bf16[64,8,4096]{2,1,0:T(8,128)(2,1)}), bf16[64,8,4096]{2,1,0:T(8,128)(2,1)}, u32[]{:S(2)}, u32[]{:S(2)}) async-start(bf16[64,8,4096]{2,1,0:T(8,128)(2,1)} %fusion.4), calls=%async_computation.2 | async-start | bytes 8388608 | tf_op jit(solution)/shard_map/all_to_all | solution.py:49
  427.8 6.2 %copy-start.1 = (f32[32,4096]{1,0:T(8,128)S(1)}, f32[32,4096]{1,0:T(8,128)}, u32[]{:S(2)}) copy-start(f32[32,4096]{1,0:T(8,128)} %reduce-scatter.2.cloned.1.call-done) | copy-start | bytes 1572868
Sparse Core Ops, SparseCore 0:
  13.6 34.7 reduce-scatter.1
  50.2 161.9 all-gather.2
  214.0 67.2 all-gather.4
where the time goes:
time: 445 us; the launch traced here: 444 us
  waiting for transfers between devices  250 us (56%)
  blocking collectives  107 us (24%)
  matrix products  57.2 us (13%)
  between operations  13.3 us (3%)
  starting transfers between devices  13 us (3%)
    all_to_all x1, blocking collectives, local(): lax.all_to_all(send_rows, 'ep', split_axis=0, concat_axis=0, tiled=True)  107 us
    all_to_all x1, waiting for transfers between devices, local(): lax.all_to_all(expert_out.reshape(ep_size, exp_local * capacity, model_wi...  101 us
    all_gather x1, waiting for transfers between devices, local(): down_full = lax.all_gather(w_down, 'tp', axis=1, tiled=True)  62 us
    all_gather x1, waiting for transfers between devices, local(): gate_up_full = lax.all_gather(w_gate_up, 'tp', axis=2, tiled=True)  53.6 us
    reduce_scatter x1, waiting for transfers between devices, local(): lax.psum_scatter(jnp.dot(context, wo_proj, preferred_element_type=jnp.flo...  31.9 us
    dot_general x8, matrix products, local(): picked = jnp.dot(picker, returned, preferred_element_type=jnp.float32)  25.1 us
    dot_general x1, matrix products, local(): jnp.einsum('sjcf,jfd->sjcd', activated, down_full, preferred_element_type...  16.6 us
    all_to_all x1, starting transfers between devices, local(): lax.all_to_all(expert_out.reshape(ep_size, exp_local * capacity, model_wi...  12.9 us
  transfers between devices with their start and end apart: 4, of which 4 were waited for; matrix products, arithmetic and copies ran while one was open for 3% of the time, Pallas kernels for 0%

commit v1 on v0

--- a/solution.py
+++ b/solution.py
@@ -2,6 +2,7 @@
 import jax.numpy as jnp
 from jax import lax
 from jax.sharding import PartitionSpec as P
+from jax.lax import all_to_all, axis_size
 
 
 def local(context, wo_proj, residual, norm_gain, expert_ids, route_weights, w_gate_up, w_down):
@@ -12,7 +13,15 @@
     experts = exp_local * ep_size
     capacity = max(2, min(quarter_rows, 2 * quarter_rows * top_count // experts))
     gate_up_full = lax.all_gather(w_gate_up, "tp", axis=2, tiled=True)
-    down_full = lax.all_gather(w_down, "tp", axis=1, tiled=True)
+    down_full = jnp.concatenate(
+        all_to_all(
+            jnp.stack([w_down for _ in range(axis_size("tp"))]),
+            axis_name="tp",
+            split_axis=0,
+            concat_axis=0,
+        ),
+        axis=1,
+    )
     attn = lax.psum_scatter(
         jnp.dot(context, wo_proj, preferred_element_type=jnp.float32),
         "tp",

time: 445 us -> 437 us (0.982)
  waiting for transfers between devices: 250 us -> 227 us
  starting transfers between devices: 13 us -> 21.8 us
    all_gather x1 -> x0, waiting for transfers between devices: 62 us -> none  [local(): down_full = lax.all_gather(w_down, 'tp', axis=1, tiled=True)]
    all_gather x1, waiting for transfers between devices: 53.6 us -> 78.9 us  [local(): gate_up_full = lax.all_gather(w_gate_up, 'tp', axis=2, tiled=True)]
    all_to_all x0 -> x1, waiting for transfers between devices: none -> 22.2 us  [local(): all_to_all(jnp.stack([w_down for _ in range(axis_size('tp'))]), axis_name...]
    all_to_all x0 -> x1, starting transfers between devices: none -> 9.29 us  [local(): all_to_all(jnp.stack([w_down for _ in range(axis_size('tp'))]), axis_name...]
    all_to_all x1, waiting for transfers between devices: 101 us -> 93 us  [local(): lax.all_to_all(expert_out.reshape(ep_size, exp_local * capacity, model_wi...]
  transfers between devices with their start and end apart: 4 -> 4, of which waited for: 4 -> 4; matrix products, arithmetic and copies ran while one was open for 3% -> 4% of each run, Pallas kernels for 0% -> 0%
where the time goes in v1:
time: 437 us; the launch traced here: 434 us
  waiting for transfers between devices  227 us (52%)
  blocking collectives  107 us (24%)
  matrix products  57.3 us (13%)
  starting transfers between devices  21.8 us (5%)
  between operations  13.6 us (3%)
  local copies, waits for them, and re-layouts  5.19 us (1%)
    all_to_all x1, blocking collectives, local(): lax.all_to_all(send_rows, 'ep', split_axis=0, concat_axis=0, tiled=True)  107 us
    all_to_all x1, waiting for transfers between devices, local(): lax.all_to_all(expert_out.reshape(ep_size, exp_local * capacity, model_wi...  93 us
    all_gather x1, waiting for transfers between devices, local(): gate_up_full = lax.all_gather(w_gate_up, 'tp', axis=2, tiled=True)  78.9 us
    reduce_scatter x1, waiting for transfers between devices, local(): lax.psum_scatter(jnp.dot(context, wo_proj, preferred_element_type=jnp.flo...  32.6 us
    dot_general x8, matrix products, local(): picked = jnp.dot(picker, returned, preferred_element_type=jnp.float32)  25.1 us
    all_to_all x1, waiting for transfers between devices, local(): all_to_all(jnp.stack([w_down for _ in range(axis_size('tp'))]), axis_name...  22.2 us
    dot_general x1, matrix products, local(): jnp.einsum('sjcf,jfd->sjcd', activated, down_full, preferred_element_type...  16.6 us
    all_to_all x1, starting transfers between devices, local(): lax.all_to_all(expert_out.reshape(ep_size, exp_local * capacity, model_wi...  12.5 us
  transfers between devices with their start and end apart: 4, of which 4 were waited for; matrix products, arithmetic and copies ran while one was open for 4% of the time, Pallas kernels for 0%

profile of v1, /device:TPU:1, one launch (start us, length us, event | category | flops | bytes accessed | tf_op | source)
XLA Modules:
  0.0 434.1 jit_solution(16740358715680958488)
XLA Ops:
  6.5 0.9 copy-done
  7.5 6.0 %fusion.41 = f32[128,4096]{1,0:T(8,128)} fusion(bf16[128,1024]{1,0:T(8,128)(2,1)S(1)} %copy-done, bf16[1024,4096]{1,0:T(8,128)(2,1)} %param.9), kind=kOutput, calls=%fused_computation.91 | convolution fusion | flops 1073741824 | bytes 10747904 | tf_op jit(solution)/shard_map/dot_general | solution.py:26
  13.6 0.7 all-gather.2.cloned.1.call-update
  14.6 0.6 reduce-window.6
  15.9 32.6 %reduce-scatter.2.cloned.1.call-done = f32[32,4096]{1,0:T(8,128)} async-done(((f32[128,4096]{1,0:T(8,128)}), f32[32,4096]{1,0:T(8,128)}) %reduce-scatter.2.cloned.1.call-update) | async-done | bytes 524304 | tf_op jit(solution)/shard_map/reduce_scatter | solution.py:25
  48.5 1.2 multiply_reduce_fusion
  49.7 2.4 fusion.2
  52.1 106.7 %all_to_all.15 = bf16[64,8,4096]{2,1,0:T(8,128)(2,1)} all-to-all(bf16[64,8,4096]{2,1,0:T(8,128)(2,1)S(1)} %fusion.2), channel_id=1, replica_groups=mesh['ep'=64,'tp'=4] {'ep'}, dimensions={0} | all-to-all | bytes 8388608 | tf_op jit(solution)/shard_map/all_to_all | solution.py:46
  158.8 3.4 stack.2
  162.2 9.3 %all-to-all-start.1 = ((bf16[4,1,192,4096]{3,2,1,0:T(8,128)(2,1)}), bf16[4,1,192,4096]{3,2,1,0:T(8,128)(2,1)}, u32[]{:S(2)}, u32[]{:S(2)}) async-start(bf16[4,1,192,4096]{3,2,1,0:T(8,128)(2,1)} %stack.2), calls=%async_computation.2 | async-start | bytes 12582912 | tf_op jit(solution)/shard_map/all_to_all | solution.py:17
  171.4 78.9 %all-gather.2.cloned.1.call-done = bf16[1,2,768,4096]{3,2,1,0:T(8,128)(2,1)} async-done(((bf16[1,2,192,4096]{3,2,1,0:T(8,128)(2,1)}), bf16[1,2,768,4096]{3,2,1,0:T(8,128)(2,1)}) %all-gather.2.cloned.1.call-update) | async-done | bytes 12582928 | tf_op jit(solution)/shard_map/all_gather | solution.py:15
  250.4 7.1 %fusion.1 = f32[64,8,768]{2,1,0:T(8,128)S(1)} fusion(bf16[64,8,4096]{2,1,0:T(8,128)(2,1)} %all_to_all.15, bf16[1,2,768,4096]{3,2,1,0:T(8,128)(2,1)} %all-gather.2.cloned.1.call-done), kind=kOutput, calls=%fused_computation.3 | convolution fusion | flops 3221225472 | bytes 12058624 | tf_op jit(solution)/shard_map/sjcd,jfd->sjcf/dot_general | solution.py:48
  257.5 22.2 %all-to-all-done.1 = bf16[4,1,192,4096]{3,2,1,0:T(8,128)(2,1)} async-done(((bf16[4,1,192,4096]{3,2,1,0:T(8,128)(2,1)}), bf16[4,1,192,4096]{3,2,1,0:T(8,128)(2,1)}, u32[]{:S(2)}, u32[]{:S(2)}) %all-to-all-start.1) | async-done | bytes 6291488 | tf_op jit(solution)/shard_map/all_to_all | solution.py:17
  279.6 16.6 %convolution_convert_fusion = bf16[64,8,4096]{2,1,0:T(8,128)(2,1)} fusion(bf16[768,4096,1]{1,0,2:T(8,128)(2,1)} %bitcast.18, bf16[64,8,4096]{2,1,0:T(8,128)(2,1)} %all_to_all.15, bf16[1,2,768,4096]{3,2,1,0:T(8,128)(2,1)} %all-gather.2.cloned.1.call-done, f32[64,8,768]{2,1,0:T(8,128)S(1)} %fusion.1), kind=kOutput, calls=%fused_computation.4 | convolution fusion | flops 6446907392 | bytes 22544384 | tf_op jit(solution)/shard_map/sjcf,jfd->sjcd/dot_general | solution.py:55
  296.3 12.5 %all-to-all-start.2 = ((bf16[64,8,4096]{2,1,0:T(8,128)(2,1)}), bf16[64,8,4096]{2,1,0:T(8,128)(2,1)}, u32[]{:S(2)}, u32[]{:S(2)}) async-start(bf16[64,8,4096]{2,1,0:T(8,128)(2,1)} %convolution_convert_fusion), calls=%async_computation.3 | async-start | bytes 8388608 | tf_op jit(solution)/shard_map/all_to_all | solution.py:58
  309.1 93.0 %all-to-all-done.2 = bf16[64,8,4096]{2,1,0:T(8,128)(2,1)} async-done(((bf16[64,8,4096]{2,1,0:T(8,128)(2,1)}), bf16[64,8,4096]{2,1,0:T(8,128)(2,1)}, u32[]{:S(2)}, u32[]{:S(2)}) %all-to-all-start.2) | async-done | bytes 4194336 | tf_op jit(solution)/shard_map/all_to_all | solution.py:58
  402.1 3.0 convolution_multiply_fusion.7
  405.1 3.0 fusion.10
  408.2 3.0 fusion.9
  411.2 3.0 fusion.8
  414.3 3.0 fusion.7
  417.3 3.1 fusion.6
  420.4 3.0 fusion.5
  423.5 3.8 fusion.11
  (31 shorter events, 1.3 us)
Async XLA Ops:
  6.5 1.0 copy-start
  6.5 41.9 %reduce-scatter.2.cloned.1.call-start = ((), (), s32[]{:S(2)}) async-start(), calls=%async_computation.4 | async-start | bytes 2621440 | tf_op jit(solution)/shard_map/reduce_scatter | solution.py:25
  13.5 0.8 copy-start.5
  13.5 2.1 copy-start.4
  13.5 35.0 %copy-start.2 = (bf16[32,4096]{1,0:T(8,128)(2,1)S(1)}, bf16[32,4096]{1,0:T(8,128)(2,1)}, u32[]{:S(2)}) copy-start(bf16[32,4096]{1,0:T(8,128)(2,1)} %param.10) | copy-start | bytes 786436
  13.5 236.9 %all-gather.2.cloned.1.call-start = ((), (), s32[]{:S(2)}) async-start(), calls=%async_computation.5 | async-start | bytes 15728640 | tf_op jit(solution)/shard_map/all_gather | solution.py:15
  52.1 106.7 %copy-start.3 = (bf16[1,192,4096]{2,1,0:T(8,128)(2,1)S(1)}, bf16[1,192,4096]{2,1,0:T(8,128)(2,1)}, u32[]{:S(2)}) copy-start(bf16[1,192,4096]{2,1,0:T(8,128)(2,1)} %param.15) | copy-start | bytes 4718596
  162.2 117.5 %all-to-all-start.1 = ((bf16[4,1,192,4096]{3,2,1,0:T(8,128)(2,1)}), bf16[4,1,192,4096]{3,2,1,0:T(8,128)(2,1)}, u32[]{:S(2)}, u32[]{:S(2)}) async-start(bf16[4,1,192,4096]{3,2,1,0:T(8,128)(2,1)} %stack.2), calls=%async_computation.2 | async-start | bytes 12582912 | tf_op jit(solution)/shard_map/all_to_all | solution.py:17
  296.3 12.8 %copy-start.6 = (f32[32,8]{0,1:T(8,128)S(1)}, f32[32,8]{0,1:T(8,128)}, u32[]{:S(2)}) copy-start(f32[32,8]{0,1:T(8,128)} %param.13) | copy-start | bytes 3076
  296.3 105.8 %all-to-all-start.2 = ((bf16[64,8,4096]{2,1,0:T(8,128)(2,1)}), bf16[64,8,4096]{2,1,0:T(8,128)(2,1)}, u32[]{:S(2)}, u32[]{:S(2)}) async-start(bf16[64,8,4096]{2,1,0:T(8,128)(2,1)} %convolution_convert_fusion), calls=%async_computation.3 | async-start | bytes 8388608 | tf_op jit(solution)/shard_map/all_to_all | solution.py:58
  417.3 6.2 %copy-start.1 = (f32[32,4096]{1,0:T(8,128)S(1)}, f32[32,4096]{1,0:T(8,128)}, u32[]{:S(2)}) copy-start(f32[32,4096]{1,0:T(8,128)} %reduce-scatter.2.cloned.1.call-done) | copy-start | bytes 1572868
Sparse Core Ops, SparseCore 0:
  13.6 34.7 reduce-scatter.1
  50.3 200.0 all-gather.1
